TPU v7x, 32 devices: a whole 2x2x4 slice. The times are simulated.
32 devices in a mesh: expert: 8 (over z, core), hidden: 4 (over y, x).
Axes of the slice: x: 2, y: 2, z: 4, core: 2. Of those that a mesh axis runs over, the one named last changes fastest.
Arguments:
- inputs: bfloat16 [1536, 2880], P('expert', 'hidden'), may hold values from -6 to 6
- out_grad: bfloat16 [1536, 2880], P('expert', 'hidden'), may hold values from -6 to 6
- expert_ids: int32 [1536, 4], P('expert'), may hold values from 0 to 7, all different within a row; in each aligned block of 192 rows (0 to 191, 192 to 383, ...) at most 144 rows name the same one
- route_weight: float32 [1536, 4], P('expert'), may hold values from 0.1 to 1
- w_gate: bfloat16 [8, 2880, 2880], P('expert', 'hidden'), may hold values from -0.109375 to 0.109375
- w_up: bfloat16 [8, 2880, 2880], P('expert', 'hidden'), may hold values from -0.109375 to 0.109375
- w_down: bfloat16 [8, 2880, 2880], P('expert', 'hidden'), may hold values from -0.109375 to 0.109375
Outputs:
- grad_input: bfloat16 [1536, 2880], P('expert', 'hidden')
- grad_route: float32 [1536, 4], P('expert')
- grad_gate: float32 [8, 2880, 2880], P('expert', 'hidden')
- grad_up: float32 [8, 2880, 2880], P('expert', 'hidden')
- grad_down: float32 [8, 2880, 2880], P('expert', 'hidden')
Inputs may be any that keep to these rules, and one draw needn't show every extreme that they name: `expert_ids`: each token names 4 different experts. Among the 192 tokens of one index of the expert axis no expert is named more than 144 times, a bound that some block reaches.
All inputs are finite; a program needn't handle non-finite values.
Results may differ from a plain program's by a relative error of at most 0.018.
Values may be sent and summed in bfloat16 or wider, within the bound.
No kernel may reach another device: no remote copies, remote signals or barrier semaphores. Data moves between devices by JAX's collectives and lax.ppermute only.
A program may use at most 128 MiB of HBM per device.

v0:
```python
import jax
import jax.numpy as jnp
from jax import lax
from jax.sharding import PartitionSpec as P


def slot_tables(expert_ids, experts, capacity):
    count, top = expert_ids.shape
    flat = expert_ids.reshape(-1)
    onehot = (flat[:, None] == jnp.arange(experts, dtype=jnp.int32)[None, :]).astype(jnp.int32)
    position = jnp.cumsum(onehot, axis=0) - 1
    slot = jnp.sum(onehot * position, axis=1)
    dest = flat * capacity + slot
    table = (
        jnp.zeros((experts * capacity,), jnp.int32)
        .at[dest]
        .set(jnp.arange(count * top, dtype=jnp.int32))
    )
    filled = jnp.zeros((experts * capacity,), jnp.int32).at[dest].set(1)
    return (dest, table, filled)


def pack_rows(values, table, filled, top, experts, capacity):
    picked = values[table // top] * filled.astype(values.dtype)[:, None]
    return picked.reshape(experts, capacity, values.shape[1])


def to_local(buffer, n_groups, local_count):
    rest = buffer.shape[2:]
    shaped = buffer.reshape((n_groups, local_count, buffer.shape[1]) + rest)
    return jnp.swapaxes(shaped, 0, 1).reshape((local_count, n_groups * buffer.shape[1]) + rest)


def from_local(buffer, n_groups, capacity):
    local_count = buffer.shape[0]
    rest = buffer.shape[2:]
    shaped = buffer.reshape((local_count, n_groups, capacity) + rest)
    return jnp.swapaxes(shaped, 0, 1).reshape((n_groups * local_count, capacity) + rest)


def per_device(inputs, out_grad, expert_ids, route_weight, w_gate, w_up, w_down):
    n_groups = lax.axis_size("expert")
    local_count = w_gate.shape[0]
    experts = local_count * n_groups
    tok_count, top = expert_ids.shape
    capacity = 3 * top * tok_count // (2 * experts)
    dest, table, filled = slot_tables(expert_ids, experts, capacity)
    send_weight = (route_weight.reshape(-1)[table] * filled.astype(jnp.float32)).reshape(
        experts, capacity
    )
    send_x = pack_rows(inputs, table, filled, top, experts, capacity)
    send_dy = pack_rows(out_grad, table, filled, top, experts, capacity)
    got_x, got_dy, got_weight = (
        lax.all_to_all(send_x, "expert", split_axis=0, concat_axis=0, tiled=True),
        lax.all_to_all(send_dy, "expert", split_axis=0, concat_axis=0, tiled=True),
        lax.all_to_all(
            send_weight.astype(jnp.bfloat16), "expert", split_axis=0, concat_axis=0, tiled=True
        ).astype(send_weight.dtype),
    )
    rows_x, rows_dy = (
        lax.all_gather(got_x, "hidden", axis=2, tiled=True),
        lax.all_gather(got_dy, "hidden", axis=2, tiled=True),
    )
    xs = to_local(rows_x, n_groups, local_count)
    dys = to_local(rows_dy, n_groups, local_count)
    weights = to_local(got_weight, n_groups, local_count)
    gate = jnp.einsum("esd,efd->esf", xs, w_gate, preferred_element_type=jnp.float32)
    up = jnp.einsum("esd,efd->esf", xs, w_up, preferred_element_type=jnp.float32)
    sig = jax.nn.sigmoid(gate)
    act = gate * sig
    hidden = (act * up).astype(jnp.bfloat16)
    back = jnp.einsum("esd,efd->esf", dys, w_down, preferred_element_type=jnp.float32)
    route_part = jnp.sum(hidden.astype(jnp.float32) * back, axis=2)
    grad_hidden = weights[:, :, None] * back
    scaled = (weights[:, :, None] * dys.astype(jnp.float32)).astype(jnp.bfloat16)
    grad_down = jnp.einsum("esf,esd->efd", hidden, scaled, preferred_element_type=jnp.float32)
    d_gate = (grad_hidden * up * sig * (1.0 + gate * (1.0 - sig))).astype(jnp.bfloat16)
    d_up = (grad_hidden * act).astype(jnp.bfloat16)
    grad_gate = jnp.einsum("esf,esd->efd", d_gate, xs, preferred_element_type=jnp.float32)
    grad_up = jnp.einsum("esf,esd->efd", d_up, xs, preferred_element_type=jnp.float32)
    partial_value = jnp.einsum("esf,efd->esd", d_gate, w_gate, preferred_element_type=jnp.float32)
    partial_value = partial_value + jnp.einsum(
        "esf,efd->esd", d_up, w_up, preferred_element_type=jnp.float32
    )
    route_total = lax.psum(route_part, "hidden")
    route_back = from_local(route_total, n_groups, capacity)
    summed = lax.psum_scatter(
        partial_value.astype(jnp.bfloat16), "hidden", scatter_dimension=2, tiled=True
    ).astype(jnp.float32)
    back_rows, back_route = (
        lax.all_to_all(
            from_local(summed, n_groups, capacity).astype(jnp.bfloat16),
            "expert",
            split_axis=0,
            concat_axis=0,
            tiled=True,
        ).astype(jnp.float32),
        lax.all_to_all(
            route_back.astype(jnp.bfloat16), "expert", split_axis=0, concat_axis=0, tiled=True
        ).astype(route_back.dtype),
    )
    per_pair = back_rows.reshape(experts * capacity, back_rows.shape[2])[dest]
    grad_input = jnp.sum(per_pair.reshape(tok_count, top, per_pair.shape[1]), axis=1).astype(
        jnp.bfloat16
    )
    grad_route = back_route.reshape(-1)[dest].reshape(tok_count, top)
    return (grad_input, grad_route, grad_gate, grad_up, grad_down)


def solution(mesh):
    placed = (
        P("expert", "hidden"),
        P("expert", "hidden"),
        P("expert", None),
        P("expert", None),
        P("expert", "hidden", None),
        P("expert", "hidden", None),
        P("expert", "hidden", None),
    )
    return jax.shard_map(
        per_device,
        mesh=mesh,
        in_specs=placed,
        out_specs=(
            P("expert", "hidden"),
            P("expert", None),
            P("expert", "hidden", None),
            P("expert", "hidden", None),
            P("expert", "hidden", None),
        ),
        check_vma=False,
    )
```

profile of v0, /device:TPU:0, one launch (start us, length us, event | category | flops | bytes accessed | tf_op | source)
XLA Modules:
  0.0 514.7 jit_solution(17609842924973014855)
XLA Ops:
  7.2 0.8 copy.50
  8.1 0.1 eq.29
  8.2 0.1 eq.25
  8.3 0.7 broadcast_multiply_fusion.2
  9.0 1.7 reduce-window.6
  10.8 0.1 copy.52
  10.9 0.2 reduce-window.9
  11.1 0.1 copy.49
  11.3 0.1 mul.98
  11.5 3.4 scatter_custom_fusion
  15.0 4.6 gather_fusion.1
  19.5 4.8 gather_fusion.2
  24.4 3.4 scatter_custom_fusion.1
  27.9 3.0 broadcast_multiply_fusion.1
  30.8 48.3 %all_to_all.27 = bf16[8,144,720]{2,1,0:T(8,128)(2,1)} all-to-all(bf16[8,144,720]{2,1,0:T(8,128)(2,1)S(1)} %get-tuple-element.32), channel_id=1, replica_groups=mesh['expert'=8,'hidden'=4] {'expert'}, dimensions={0} | all-to-all | bytes 3317760 | tf_op jit(solution)/shard_map/all_to_all | solution.py:54
  79.1 5.1 copy.57
  84.3 45.2 %all_to_all.28 = bf16[8,144,720]{2,1,0:T(8,128)(2,1)} all-to-all(bf16[8,144,720]{2,1,0:T(8,128)(2,1)S(1)} %copy-done.3), channel_id=1, replica_groups=mesh['expert'=8,'hidden'=4] {'expert'}, dimensions={0} | all-to-all | bytes 3317760 | tf_op jit(solution)/shard_map/all_to_all | solution.py:55
  129.4 5.0 copy.55
  134.5 0.1 copy.48
  134.6 0.1 reshape.221
  134.8 4.6 gather_fusion
  139.4 8.0 %all_to_all.29 = bf16[8,1,144]{2,1,0:T(2,128)(2,1)S(1)} all-to-all(bf16[8,1,144]{2,1,0:T(2,128)(2,1)S(1)} %convert_element_type.129), channel_id=1, replica_groups=mesh['expert'=8,'hidden'=4] {'expert'}, dimensions={0} | all-to-all | bytes 4608 | tf_op jit(solution)/shard_map/all_to_all | solution.py:56
  147.5 51.6 %all-gather.5.cloned.1.call-done = bf16[8,144,2880]{1,0,2:T(8,128)(2,1)} async-done(((bf16[8,144,720]{1,0,2:T(8,128)(2,1)}), bf16[8,144,2880]{1,0,2:T(8,128)(2,1)}) %all-gather.5.cloned.1.call-update) | async-done | bytes 6635536 | tf_op jit(solution)/shard_map/all_gather | solution.py:61
  199.1 16.3 %copy.58 = bf16[8,144,2880]{2,1,0:T(8,128)(2,1)} copy(bf16[8,144,2880]{1,0,2:T(8,128)(2,1)} %all-gather.5.cloned.1.call-done) | data formatting | bytes 13271040 | tf_op jit(solution)/shard_map/all_gather | solution.py:61
  215.4 11.0 %fusion.10 = f32[1152,720]{0,1:T(8,128)} fusion(bf16[1152,2880]{1,0:T(8,128)(2,1)} %bitcast.60, bf16[1,720,2880]{2,1,0:T(8,128)(2,1)} %param.12), kind=kOutput, calls=%fused_computation.21 | convolution fusion | flops 4777574400 | bytes 14100480 | tf_op jit(solution)/shard_map/esd,efd->esf/dot_general | solution.py:68
  226.4 7.6 %fusion.7 = f32[1152,720]{0,1:T(8,128)} fusion(bf16[1152,2880]{1,0:T(8,128)(2,1)S(1)} %bitcast.63, bf16[1,720,2880]{2,1,0:T(8,128)(2,1)S(1)} %bitcast.69), kind=kOutput, calls=%fused_computation.18 | convolution fusion | flops 4777574400 | bytes 14100480 | tf_op jit(solution)/shard_map/esd,efd->esf/dot_general | solution.py:67
  234.0 82.8 %all-gather.3.cloned.1.call-done = bf16[8,144,2880]{1,0,2:T(8,128)(2,1)} async-done(((bf16[8,144,720]{1,0,2:T(8,128)(2,1)}), bf16[8,144,2880]{1,0,2:T(8,128)(2,1)}) %all-gather.3.cloned.1.call-update) | async-done | bytes 6635536 | tf_op jit(solution)/shard_map/all_gather | solution.py:62
  316.9 15.4 %copy.56 = bf16[8,144,2880]{2,1,0:T(8,128)(2,1)} copy(bf16[8,144,2880]{1,0,2:T(8,128)(2,1)} %all-gather.3.cloned.1.call-done) | data formatting | bytes 13271040 | tf_op jit(solution)/shard_map/all_gather | solution.py:62
  332.2 13.6 %multiply_reduce_fusion = (f32[1152]{0:T(1024)S(1)}, bf16[1152,720]{0,1:T(8,128)(2,1)}, bf16[1152,720]{0,1:T(8,128)(2,1)S(1)}, bf16[1152,720]{0,1:T(8,128)(2,1)}) fusion(f32[1152,720]{0,1:T(8,128)} %fusion.10, f32[1152,720]{0,1:T(8,128)} %fusion.7, f32[1152]{0:T(1024)S(1)} %reshape.232, bf16[1152,2880]{1,0:T(8,128)(2,1)} %bitcast.64, ...), kind=kOutput, calls=%fused_computation.25 | convolution fusion | flops 4793332736 | bytes 22404096 | tf_op jit(solution)/shard_map/esd,efd->esf/dot_general | solution.py:72
  345.9 8.8 %fusion.5 = f32[1152,2880]{0,1:T(8,128)} fusion(bf16[1152,720]{0,1:T(8,128)(2,1)S(1)} %get-tuple-element.27, bf16[1,720,2880]{2,1,0:T(8,128)(2,1)S(1)} %bitcast.71), kind=kOutput, calls=%fused_computation.16 | convolution fusion | flops 4777574400 | bytes 19077120 | tf_op jit(solution)/shard_map/esf,efd->esd/dot_general | solution.py:81
  354.6 15.3 %fusion.1 = bf16[1,1152,2880]{1,2,0:T(8,128)(2,1)} fusion(f32[1152,2880]{0,1:T(8,128)} %fusion.5, bf16[1152,720]{0,1:T(8,128)(2,1)} %get-tuple-element.28, bf16[1,720,2880]{2,1,0:T(8,128)(2,1)} %param.12), kind=kOutput, calls=%fused_computation.10 | convolution fusion | flops 4784209920 | bytes 25712640 | tf_op jit(solution)/shard_map/esf,efd->esd/dot_general | solution.py:82
  370.0 16.9 %psum.7 = bf16[1,1152]{1,0:T(2,128)(2,1)S(1)} all-reduce(f32[1,1152]{1,0:T(1,128)S(1)} %reduce_sum.35), channel_id=1, replica_groups=mesh['expert'=8,'hidden'=4] {'hidden'}, use_global_device_ids=true, to_apply=%region_8.9 | all-reduce | flops 1152 | bytes 6912 | tf_op jit(solution)/shard_map/psum | solution.py:85
  386.9 0.7 convert_element_type.130
  387.6 4.6 all-to-all-start.4
  392.2 11.6 %convolution_bitcast_fusion = f32[1,720,2880]{2,1,0:T(8,128)} fusion(bf16[1152,720]{0,1:T(8,128)(2,1)S(1)} %copy-done.7, bf16[1152,2880]{1,0:T(8,128)(2,1)} %bitcast.61), kind=kOutput, calls=%fused_computation.14 | convolution fusion | flops 4777574400 | bytes 16588800 | tf_op jit(solution)/shard_map/esf,esd->efd/dot_general | solution.py:80
  403.8 40.7 %reduce-scatter.7.cloned.1.call-done = bf16[1,1152,720]{1,2,0:T(8,128)(2,1)} async-done(((bf16[1,1152,2880]{1,2,0:T(8,128)(2,1)}), bf16[1,1152,720]{1,2,0:T(8,128)(2,1)}) %reduce-scatter.7.cloned.1.call-update) | async-done | bytes 1658896
  444.6 3.8 copy.59
  448.4 4.6 all-to-all-start.3
  452.9 11.4 %convolution_bitcast_fusion.1 = f32[1,720,2880]{2,1,0:T(8,128)} fusion(bf16[1152,720]{0,1:T(8,128)(2,1)} %copy-done.6, bf16[1152,2880]{1,0:T(8,128)(2,1)} %bitcast.62), kind=kOutput, calls=%fused_computation.15 | convolution fusion | flops 4777574400 | bytes 16588800 | tf_op jit(solution)/shard_map/esf,esd->efd/dot_general | solution.py:79
  464.3 11.2 %fusion.4 = f32[1,720,2880]{2,1,0:T(8,128)} fusion(bf16[1152,720]{0,1:T(8,128)(2,1)S(1)} %copy-done.8, bf16[1152,2880]{1,0:T(8,128)(2,1)} %bitcast.65, f32[1152]{0:T(1024)S(1)} %reshape.232), kind=kOutput, calls=%fused_computation.13 | convolution fusion | flops 4787527680 | bytes 16593408 | tf_op jit(solution)/shard_map/esf,esd->efd/dot_general | solution.py:76
  475.7 4.5 gather_fusion.4
  480.2 0.1 reshape.231
  480.3 0.7 copy.61
  480.9 14.0 %all-to-all-done.3 = bf16[8,144,720]{2,1,0:T(8,128)(2,1)S(1)} async-done(((bf16[8,144,720]{2,1,0:T(8,128)(2,1)}), bf16[8,144,720]{2,1,0:T(8,128)(2,1)S(1)}, u32[]{:S(2)}, u32[]{:S(2)}) %all-to-all-start.3) | async-done | bytes 1658912 | tf_op jit(solution)/shard_map/all_to_all | solution.py:91
  495.0 2.1 bitcast_convert_fusion
  497.1 6.1 %gather_fusion.3 = f32[768,720]{1,0:T(8,128)} fusion(f32[1152,720]{1,0:T(8,128)} %bitcast_convert_fusion, s32[1024]{0:T(1024)S(1)} %pad_clamp_fusion.2), kind=kCustom, calls=%fused_computation.3 | custom fusion | bytes 4426752 | tf_op jit(solution)/shard_map/gather | solution.py:102
  503.2 2.6 reshape.230
  505.8 2.3 reduce_sum.33
  (55 shorter events, 1.0 us)
Async XLA Ops:
  7.2 7.8 %copy-start = (bf16[192,720]{1,0:T(8,128)(2,1)S(1)}, bf16[192,720]{1,0:T(8,128)(2,1)}, u32[]{:S(2)}) copy-start(bf16[192,720]{1,0:T(8,128)(2,1)} %param.8) | copy-start | bytes 829444
  7.2 192.0 %all-gather.5.cloned.1.call-start = ((), (), s32[]{:S(2)}) async-start(), calls=%async_computation.7 | async-start | bytes 14745600 | tf_op jit(solution)/shard_map/all_gather | solution.py:61
  15.0 4.6 copy-start.2
  79.1 5.2 %copy-start.3 = (bf16[8,144,720]{2,1,0:T(8,128)(2,1)S(1)}, bf16[8,144,720]{2,1,0:T(8,128)(2,1)}, u32[]{:S(2)}) copy-start(bf16[8,144,720]{2,1,0:T(8,128)(2,1)} %get-tuple-element.31) | copy-start | bytes 4976644
  84.2 232.6 %all-gather.3.cloned.1.call-start = ((), (), s32[]{:S(2)}) async-start(), calls=%async_computation.6 | async-start | bytes 14745600 | tf_op jit(solution)/shard_map/all_gather | solution.py:62
  129.4 5.1 copy-start.5
  134.5 310.1 %reduce-scatter.7.cloned.1.call-start = ((), (), s32[]{:S(2)}) async-start(), calls=%async_computation.8 | async-start | bytes 8294400
  199.1 27.3 %slice-start = ((s8[4239360]{0:T(1024)(128)(4,1)}), s8[45056]{0:T(1024)(128)(4,1)S(1)}, s32[]{:S(2)}) async-start(s8[4239360]{0:T(1024)(128)(4,1)} %bitcast.68), calls=%async_computation.9 | async-start | bytes 90112
  215.4 11.0 %copy-start.4 = (bf16[8,144,2880]{2,1,0:T(8,128)(2,1)S(1)}, bf16[8,144,2880]{2,1,0:T(8,128)(2,1)}, u32[]{:S(2)}) copy-start(bf16[8,144,2880]{2,1,0:T(8,128)(2,1)} %copy.58) | copy-start | bytes 19906564
  215.4 11.0 %slice-start.1 = ((s8[4239360]{0:T(1024)(128)(4,1)}), s8[4194304]{0:T(1024)(128)(4,1)S(1)}, s32[]{:S(2)}) async-start(s8[4239360]{0:T(1024)(128)(4,1)} %bitcast.68), calls=%async_computation.10 | async-start | bytes 8388608
  316.9 29.0 %slice-start.2 = ((s8[4239360]{0:T(1024)(128)(4,1)}), s8[45056]{0:T(1024)(128)(4,1)S(1)}, s32[]{:S(2)}) async-start(s8[4239360]{0:T(1024)(128)(4,1)} %bitcast.70), calls=%async_computation.11 | async-start | bytes 90112
  332.2 13.6 %slice-start.3 = ((s8[4239360]{0:T(1024)(128)(4,1)}), s8[4194304]{0:T(1024)(128)(4,1)S(1)}, s32[]{:S(2)}) async-start(s8[4239360]{0:T(1024)(128)(4,1)} %bitcast.70), calls=%async_computation.12 | async-start | bytes 8388608
  345.8 8.8 %copy-start.6 = (bf16[1152,720]{0,1:T(8,128)(2,1)}, bf16[1152,720]{0,1:T(8,128)(2,1)S(1)}, u32[]{:S(2)}) copy-start(bf16[1152,720]{0,1:T(8,128)(2,1)S(1)} %get-tuple-element.27) | copy-start | bytes 4976644
  370.0 22.3 %copy-start.7 = (bf16[1152,720]{0,1:T(8,128)(2,1)S(1)}, bf16[1152,720]{0,1:T(8,128)(2,1)}, u32[]{:S(2)}) copy-start(bf16[1152,720]{0,1:T(8,128)(2,1)} %get-tuple-element.28) | copy-start | bytes 4976644
  387.6 60.7 %all-to-all-start.4 = ((bf16[8,1,144]{2,1,0:T(2,128)(2,1)}), bf16[8,1,144]{2,1,0:T(2,128)(2,1)S(1)}, u32[]{:S(2)}, u32[]{:S(2)}) async-start(bf16[8,1,144]{2,1,0:T(2,128)(2,1)} %convert_element_type.130), calls=%async_computation.4 | async-start | bytes 16384 | tf_op jit(solution)/shard_map/all_to_all | solution.py:98
  448.4 46.6 %all-to-all-start.3 = ((bf16[8,144,720]{2,1,0:T(8,128)(2,1)}), bf16[8,144,720]{2,1,0:T(8,128)(2,1)S(1)}, u32[]{:S(2)}, u32[]{:S(2)}) async-start(bf16[8,144,720]{2,1,0:T(8,128)(2,1)} %bitcast.11), calls=%async_computation.3 | async-start | bytes 3538944 | tf_op jit(solution)/shard_map/all_to_all | solution.py:91
  452.9 11.4 %copy-start.8 = (bf16[1152,720]{0,1:T(8,128)(2,1)S(1)}, bf16[1152,720]{0,1:T(8,128)(2,1)}, u32[]{:S(2)}) copy-start(bf16[1152,720]{0,1:T(8,128)(2,1)} %get-tuple-element.26) | copy-start | bytes 4976644
  497.1 11.1 %copy-start.1 = (bf16[192,720]{1,0:T(8,128)(2,1)S(1)}, bf16[192,720]{1,0:T(8,128)(2,1)}, u32[]{:S(2)}) copy-start(bf16[192,720]{1,0:T(8,128)(2,1)} %param.8) | copy-start | bytes 829444
Sparse Core Ops, SparseCore 0:
  84.3 114.7 all-gather.4
  201.0 115.8 all-gather.2
  370.1 74.3 reduce-scatter.6
where the time goes:
time: 516 us; the launch traced here: 515 us
  waiting for transfers between devices  189 us (37%)
  blocking collectives  118 us (23%)
  matrix products  90.5 us (18%)
  local copies, waits for them, and re-layouts  83.2 us (16%)
  between operations  14 us (3%)
  other arithmetic  10.2 us (2%)
  starting transfers between devices  9.32 us (2%)
    all_gather x1, waiting for transfers between devices, per_device(): lax.all_gather(got_dy, 'hidden', axis=2, tiled=True)  82.8 us
    all_gather x1, waiting for transfers between devices, per_device(): lax.all_gather(got_x, 'hidden', axis=2, tiled=True)  51.6 us
    all_to_all x1, blocking collectives, per_device(): lax.all_to_all(send_x, 'expert', split_axis=0, concat_axis=0, tiled=True)  48.3 us
    all_to_all x1, blocking collectives, per_device(): lax.all_to_all(send_dy, 'expert', split_axis=0, concat_axis=0, tiled=True)  45.2 us
    unnamed x4, waiting for transfers between devices  40.8 us
    psum x1, blocking collectives, per_device(): route_total = lax.psum(route_part, 'hidden')  16.9 us
    all_gather x1, local copies, waits for them, and re-layouts, per_device(): lax.all_gather(got_x, 'hidden', axis=2, tiled=True)  16.3 us
    all_gather x1, local copies, waits for them, and re-layouts, per_device(): lax.all_gather(got_dy, 'hidden', axis=2, tiled=True)  15.4 us
  transfers between devices with their start and end apart: 5, of which 4 were waited for; matrix products, arithmetic and copies ran while one was open for 17% of the time, Pallas kernels for 0%

commit v1 on v0

--- a/solution.py
+++ b/solution.py
@@ -59,7 +59,7 @@
     )
     rows_x, rows_dy = (
         lax.all_gather(got_x, "hidden", axis=2, tiled=True),
-        lax.all_gather(got_dy, "hidden", axis=2, tiled=True),
+        jnp.concatenate(lax.all_gather(got_dy, "hidden"), axis=2),
     )
     xs = to_local(rows_x, n_groups, local_count)
     dys = to_local(rows_dy, n_groups, local_count)

time: 516 us -> 490 us (0.950)
  waiting for transfers between devices: 189 us -> 155 us
    all_gather x1, waiting for transfers between devices: 82.8 us -> 44 us  [per_device(): lax.all_gather(got_dy, 'hidden')]
    all_gather x1 -> x0, local copies, waits for them, and re-layouts: 15.4 us -> none  [per_device(): lax.all_gather(got_dy, 'hidden', axis=2, tiled=True)]
    another operation x1 -> x2, local copies, waits for them, and re-layouts: 0.08 us -> 13.9 us
    reshape x0 -> x1, local copies, waits for them, and re-layouts: none -> 11.4 us  [per_device(): jnp.concatenate(lax.all_gather(got_dy, 'hidden'), axis=2)]
where the time goes in v1:
time: 490 us; the launch traced here: 484 us
  waiting for transfers between devices  155 us (32%)
  blocking collectives  119 us (24%)
  matrix products  88.6 us (18%)
  local copies, waits for them, and re-layouts  87.6 us (18%)
  between operations  14.3 us (3%)
  other arithmetic  10.2 us (2%)
  starting transfers between devices  9.52 us (2%)
    all_gather x1, waiting for transfers between devices, per_device(): lax.all_gather(got_x, 'hidden', axis=2, tiled=True)  56.4 us
    all_to_all x1, blocking collectives, per_device(): lax.all_to_all(send_x, 'expert', split_axis=0, concat_axis=0, tiled=True)  48.3 us
    all_to_all x1, blocking collectives, per_device(): lax.all_to_all(send_dy, 'expert', split_axis=0, concat_axis=0, tiled=True)  45.2 us
    all_gather x1, waiting for transfers between devices, per_device(): lax.all_gather(got_dy, 'hidden')  44 us
    unnamed x4, waiting for transfers between devices  40.7 us
    psum x1, blocking collectives, per_device(): route_total = lax.psum(route_part, 'hidden')  16.9 us
    all_gather x1, local copies, waits for them, and re-layouts, per_device(): lax.all_gather(got_x, 'hidden', axis=2, tiled=True)  15.8 us
    all_to_all x1, waiting for transfers between devices, per_device(): lax.all_to_all(from_local(summed, n_groups, capacity).astype(jnp.bfloat16...  14 us
  transfers between devices with their start and end apart: 5, of which 4 were waited for; matrix products, arithmetic and copies ran while one was open for 17% of the time, Pallas kernels for 0%

profile of v1, /device:TPU:0, one launch (start us, length us, event | category | flops | bytes accessed | tf_op | source)
XLA Modules:
  0.0 483.7 jit_solution(3125901976314431543)
XLA Ops:
  7.2 0.7 broadcast_multiply_fusion.2
  8.0 0.8 copy.45
  8.8 0.1 eq.29
  8.9 0.1 eq.25
  9.0 0.1 copy.44
  9.1 0.1 mul.98
  9.2 1.7 reduce-window.6
  11.0 0.1 copy.47
  11.2 0.2 reduce-window.9
  11.5 3.4 scatter_custom_fusion
  15.0 3.4 scatter_custom_fusion.1
  18.5 4.6 gather_fusion.1
  23.1 4.8 gather_fusion.2
  27.9 3.0 broadcast_multiply_fusion.1
  30.9 48.3 %all_to_all.27 = bf16[8,144,720]{2,1,0:T(8,128)(2,1)} all-to-all(bf16[8,144,720]{2,1,0:T(8,128)(2,1)S(1)} %get-tuple-element.32), channel_id=1, replica_groups=mesh['expert'=8,'hidden'=4] {'expert'}, dimensions={0} | all-to-all | bytes 3317760 | tf_op jit(solution)/shard_map/all_to_all | solution.py:54
  79.1 5.1 %copy.51 = bf16[8,144,720]{1,0,2:T(8,128)(2,1)} copy(bf16[8,144,720]{2,1,0:T(8,128)(2,1)} %all_to_all.27) | data formatting | bytes 3317760 | tf_op jit(solution)/shard_map/all_to_all | solution.py:54
  84.3 45.2 %all_to_all.28 = bf16[8,144,720]{2,1,0:T(8,128)(2,1)} all-to-all(bf16[8,144,720]{2,1,0:T(8,128)(2,1)S(1)} %copy-done.3), channel_id=1, replica_groups=mesh['expert'=8,'hidden'=4] {'expert'}, dimensions={0} | all-to-all | bytes 3317760 | tf_op jit(solution)/shard_map/all_to_all | solution.py:55
  129.6 0.1 copy.43
  129.7 0.1 reshape.224
  129.8 4.6 gather_fusion
  134.5 8.2 %all_to_all.29 = bf16[8,1,144]{2,1,0:T(2,128)(2,1)S(1)} all-to-all(bf16[8,1,144]{2,1,0:T(2,128)(2,1)S(1)} %convert_element_type.129), channel_id=1, replica_groups=mesh['expert'=8,'hidden'=4] {'expert'}, dimensions={0} | all-to-all | bytes 4608 | tf_op jit(solution)/shard_map/all_to_all | solution.py:56
  142.8 56.4 %all-gather.4.cloned.1.call-done = bf16[8,144,2880]{1,0,2:T(8,128)(2,1)} async-done(((bf16[8,144,720]{1,0,2:T(8,128)(2,1)}), bf16[8,144,2880]{1,0,2:T(8,128)(2,1)}) %all-gather.4.cloned.1.call-update) | async-done | bytes 6635536 | tf_op jit(solution)/shard_map/all_gather | solution.py:61
  199.2 15.8 %copy.52 = bf16[8,144,2880]{2,1,0:T(8,128)(2,1)} copy(bf16[8,144,2880]{1,0,2:T(8,128)(2,1)} %all-gather.4.cloned.1.call-done) | data formatting | bytes 13271040 | tf_op jit(solution)/shard_map/all_gather | solution.py:61
  215.0 11.0 %fusion.10 = f32[1152,720]{0,1:T(8,128)} fusion(bf16[1152,2880]{1,0:T(8,128)(2,1)} %bitcast.63, bf16[1,720,2880]{2,1,0:T(8,128)(2,1)} %param.12), kind=kOutput, calls=%fused_computation.21 | convolution fusion | flops 4777574400 | bytes 14100480 | tf_op jit(solution)/shard_map/esd,efd->esf/dot_general | solution.py:68
  226.0 7.6 %fusion.7 = f32[1152,720]{0,1:T(8,128)} fusion(bf16[1152,2880]{1,0:T(8,128)(2,1)S(1)} %bitcast.66, bf16[1,720,2880]{2,1,0:T(8,128)(2,1)S(1)} %bitcast.70), kind=kOutput, calls=%fused_computation.18 | convolution fusion | flops 4777574400 | bytes 14100480 | tf_op jit(solution)/shard_map/esd,efd->esf/dot_general | solution.py:67
  233.6 44.0 %all-gather.6.cloned.1.call-done = bf16[32,144,720]{2,1,0:T(8,128)(2,1)} async-done(((bf16[8,144,720]{2,1,0:T(8,128)(2,1)}), bf16[32,144,720]{2,1,0:T(8,128)(2,1)}) %all-gather.6.cloned.1.call-update) | async-done | bytes 6635536 | tf_op jit(solution)/shard_map/all_gather | solution.py:62
  277.6 11.4 %copy.50 = bf16[8,144,4,720]{3,2,1,0:T(4,128)(2,1)} copy(bf16[8,144,4,720]{3,1,0,2:T(8,128)(2,1)} %bitcast.62) | data formatting | bytes 13271040 | tf_op jit(solution)/shard_map/reshape | solution.py:62
  289.1 13.8 %reshape.227 = bf16[1152,2880]{1,0:T(8,128)(2,1)} reshape(bf16[8,144,4,720]{3,2,1,0:T(4,128)(2,1)} %copy.50) | data formatting | bytes 13271040 | tf_op jit(solution)/shard_map/reshape.4
  302.8 13.9 %multiply_reduce_fusion = (f32[1152]{0:T(1024)S(1)}, bf16[1152,720]{0,1:T(8,128)(2,1)}, bf16[1152,720]{0,1:T(8,128)(2,1)S(1)}, bf16[1152,720]{0,1:T(8,128)(2,1)S(1)}) fusion(f32[1152,720]{0,1:T(8,128)} %fusion.10, f32[1152,720]{0,1:T(8,128)} %fusion.7, f32[1152]{0:T(1024)S(1)} %reshape.236, bf16[1152,2880]{1,0:T(8,128)(2,1)} %reshape.227, ...), kind=kOutput, calls=%fused_computation.25 | convolution fusion | flops 4793332736 | bytes 22404096 | tf_op jit(solution)/shard_map/esd,efd->esf/dot_general | solution.py:72
  316.7 8.9 %fusion.5 = f32[1152,2880]{0,1:T(8,128)} fusion(bf16[1152,720]{0,1:T(8,128)(2,1)S(1)} %get-tuple-element.27, bf16[1,720,2880]{2,1,0:T(8,128)(2,1)S(1)} %bitcast.72), kind=kOutput, calls=%fused_computation.16 | convolution fusion | flops 4777574400 | bytes 19077120 | tf_op jit(solution)/shard_map/esf,efd->esd/dot_general | solution.py:81
  325.6 13.0 %fusion.1 = bf16[1,1152,2880]{1,2,0:T(8,128)(2,1)} fusion(f32[1152,2880]{0,1:T(8,128)} %fusion.5, bf16[1152,720]{0,1:T(8,128)(2,1)S(1)} %get-tuple-element.28, bf16[1,720,2880]{2,1,0:T(8,128)(2,1)} %param.12), kind=kOutput, calls=%fused_computation.10 | convolution fusion | flops 4784209920 | bytes 25712640 | tf_op jit(solution)/shard_map/esf,efd->esd/dot_general | solution.py:82
  338.7 16.9 %psum.7 = bf16[1,1152]{1,0:T(2,128)(2,1)S(1)} all-reduce(f32[1,1152]{1,0:T(1,128)S(1)} %reduce_sum.35), channel_id=1, replica_groups=mesh['expert'=8,'hidden'=4] {'hidden'}, use_global_device_ids=true, to_apply=%region_8.9 | all-reduce | flops 1152 | bytes 6912 | tf_op jit(solution)/shard_map/psum | solution.py:85
  355.6 0.7 convert_element_type.130
  356.3 4.6 all-to-all-start.4
  360.9 11.6 %convolution_bitcast_fusion.1 = f32[1,720,2880]{2,1,0:T(8,128)} fusion(bf16[1152,720]{0,1:T(8,128)(2,1)S(1)} %copy-done.8, bf16[1152,2880]{1,0:T(8,128)(2,1)} %bitcast.64), kind=kOutput, calls=%fused_computation.15 | convolution fusion | flops 4777574400 | bytes 16588800 | tf_op jit(solution)/shard_map/esf,esd->efd/dot_general | solution.py:79
  372.5 40.7 %reduce-scatter.7.cloned.1.call-done = bf16[1,1152,720]{1,2,0:T(8,128)(2,1)} async-done(((bf16[1,1152,2880]{1,2,0:T(8,128)(2,1)}), bf16[1,1152,720]{1,2,0:T(8,128)(2,1)}) %reduce-scatter.7.cloned.1.call-update) | async-done | bytes 1658896
  413.2 3.8 copy.53
  417.1 4.8 all-to-all-start.3
  421.9 11.4 %convolution_bitcast_fusion = f32[1,720,2880]{2,1,0:T(8,128)} fusion(bf16[1152,720]{0,1:T(8,128)(2,1)} %copy-done.6, bf16[1152,2880]{1,0:T(8,128)(2,1)} %bitcast.65), kind=kOutput, calls=%fused_computation.14 | convolution fusion | flops 4777574400 | bytes 16588800 | tf_op jit(solution)/shard_map/esf,esd->efd/dot_general | solution.py:80
  433.2 11.2 %fusion.4 = f32[1,720,2880]{2,1,0:T(8,128)} fusion(bf16[1152,720]{0,1:T(8,128)(2,1)S(1)} %copy-done.9, bf16[1152,2880]{1,0:T(8,128)(2,1)} %reshape.227, f32[1152]{0:T(1024)S(1)} %reshape.236), kind=kOutput, calls=%fused_computation.13 | convolution fusion | flops 4787527680 | bytes 16593408 | tf_op jit(solution)/shard_map/esf,esd->efd/dot_general | solution.py:76
  444.6 4.5 gather_fusion.4
  449.1 0.1 reshape.235
  449.2 0.7 copy.55
  449.9 14.0 %all-to-all-done.3 = bf16[8,144,720]{2,1,0:T(8,128)(2,1)S(1)} async-done(((bf16[8,144,720]{2,1,0:T(8,128)(2,1)}), bf16[8,144,720]{2,1,0:T(8,128)(2,1)S(1)}, u32[]{:S(2)}, u32[]{:S(2)}) %all-to-all-start.3) | async-done | bytes 1658912 | tf_op jit(solution)/shard_map/all_to_all | solution.py:91
  463.8 2.1 bitcast_convert_fusion
  466.0 6.1 %gather_fusion.3 = f32[768,720]{1,0:T(8,128)} fusion(f32[1152,720]{1,0:T(8,128)} %bitcast_convert_fusion, s32[1024]{0:T(1024)S(1)} %pad_clamp_fusion.2), kind=kCustom, calls=%fused_computation.3 | custom fusion | bytes 4426752 | tf_op jit(solution)/shard_map/gather | solution.py:102
  472.1 2.6 reshape.234
  474.7 2.3 reduce_sum.33
  (57 shorter events, 1.0 us)
Async XLA Ops:
  7.2 11.3 %copy-start = (bf16[192,720]{1,0:T(8,128)(2,1)S(1)}, bf16[192,720]{1,0:T(8,128)(2,1)}, u32[]{:S(2)}) copy-start(bf16[192,720]{1,0:T(8,128)(2,1)} %param.8) | copy-start | bytes 829444
  7.2 192.0 %all-gather.4.cloned.1.call-start = ((), (), s32[]{:S(2)}) async-start(), calls=%async_computation.6 | async-start | bytes 14745600 | tf_op jit(solution)/shard_map/all_gather | solution.py:61
  18.5 4.6 copy-start.2
  79.1 5.2 %copy-start.3 = (bf16[8,144,720]{2,1,0:T(8,128)(2,1)S(1)}, bf16[8,144,720]{2,1,0:T(8,128)(2,1)}, u32[]{:S(2)}) copy-start(bf16[8,144,720]{2,1,0:T(8,128)(2,1)} %get-tuple-element.31) | copy-start | bytes 4976644
  84.2 45.3 %copy-start.5 = (f32[192,4]{0,1:T(4,128)S(1)}, f32[192,4]{0,1:T(4,128)}, u32[]{:S(2)}) copy-start(f32[192,4]{0,1:T(4,128)} %param.10) | copy-start | bytes 9220
  84.3 193.4 %all-gather.6.cloned.1.call-start = ((), (), s32[]{:S(2)}) async-start(), calls=%async_computation.7 | async-start | bytes 8847360 | tf_op jit(solution)/shard_map/all_gather | solution.py:62
  129.5 283.7 %reduce-scatter.7.cloned.1.call-start = ((), (), s32[]{:S(2)}) async-start(), calls=%async_computation.8 | async-start | bytes 8294400
  199.2 26.8 %slice-start = ((s8[4239360]{0:T(1024)(128)(4,1)}), s8[45056]{0:T(1024)(128)(4,1)S(1)}, s32[]{:S(2)}) async-start(s8[4239360]{0:T(1024)(128)(4,1)} %bitcast.69), calls=%async_computation.9 | async-start | bytes 90112
  215.0 11.0 %copy-start.4 = (bf16[8,144,2880]{2,1,0:T(8,128)(2,1)S(1)}, bf16[8,144,2880]{2,1,0:T(8,128)(2,1)}, u32[]{:S(2)}) copy-start(bf16[8,144,2880]{2,1,0:T(8,128)(2,1)} %copy.52) | copy-start | bytes 19906564
  215.0 11.0 %slice-start.1 = ((s8[4239360]{0:T(1024)(128)(4,1)}), s8[4194304]{0:T(1024)(128)(4,1)S(1)}, s32[]{:S(2)}) async-start(s8[4239360]{0:T(1024)(128)(4,1)} %bitcast.69), calls=%async_computation.10 | async-start | bytes 8388608
  289.0 27.7 %slice-start.2 = ((s8[4239360]{0:T(1024)(128)(4,1)}), s8[45056]{0:T(1024)(128)(4,1)S(1)}, s32[]{:S(2)}) async-start(s8[4239360]{0:T(1024)(128)(4,1)} %bitcast.71), calls=%async_computation.11 | async-start | bytes 90112
  302.8 13.9 %slice-start.3 = ((s8[4239360]{0:T(1024)(128)(4,1)}), s8[4194304]{0:T(1024)(128)(4,1)S(1)}, s32[]{:S(2)}) async-start(s8[4239360]{0:T(1024)(128)(4,1)} %bitcast.71), calls=%async_computation.12 | async-start | bytes 8388608
  316.7 8.9 %copy-start.7 = (bf16[1152,720]{0,1:T(8,128)(2,1)}, bf16[1152,720]{0,1:T(8,128)(2,1)S(1)}, u32[]{:S(2)}) copy-start(bf16[1152,720]{0,1:T(8,128)(2,1)S(1)} %get-tuple-element.27) | copy-start | bytes 4976644
  316.7 8.9 %copy-start.6 = (bf16[1152,720]{0,1:T(8,128)(2,1)}, bf16[1152,720]{0,1:T(8,128)(2,1)S(1)}, u32[]{:S(2)}) copy-start(bf16[1152,720]{0,1:T(8,128)(2,1)S(1)} %get-tuple-element.28) | copy-start | bytes 4976644
  338.7 22.3 %copy-start.8 = (bf16[1152,720]{0,1:T(8,128)(2,1)S(1)}, bf16[1152,720]{0,1:T(8,128)(2,1)}, u32[]{:S(2)}) copy-start(bf16[1152,720]{0,1:T(8,128)(2,1)} %copy-done.7) | copy-start | bytes 4976644
  356.3 60.7 %all-to-all-start.4 = ((bf16[8,1,144]{2,1,0:T(2,128)(2,1)}), bf16[8,1,144]{2,1,0:T(2,128)(2,1)S(1)}, u32[]{:S(2)}, u32[]{:S(2)}) async-start(bf16[8,1,144]{2,1,0:T(2,128)(2,1)} %convert_element_type.130), calls=%async_computation.4 | async-start | bytes 16384 | tf_op jit(solution)/shard_map/all_to_all | solution.py:98
  417.1 46.8 %all-to-all-start.3 = ((bf16[8,144,720]{2,1,0:T(8,128)(2,1)}), bf16[8,144,720]{2,1,0:T(8,128)(2,1)S(1)}, u32[]{:S(2)}, u32[]{:S(2)}) async-start(bf16[8,144,720]{2,1,0:T(8,128)(2,1)} %bitcast.12), calls=%async_computation.3 | async-start | bytes 3538944 | tf_op jit(solution)/shard_map/all_to_all | solution.py:91
  421.9 11.4 %copy-start.9 = (bf16[1152,720]{0,1:T(8,128)(2,1)S(1)}, bf16[1152,720]{0,1:T(8,128)(2,1)}, u32[]{:S(2)}) copy-start(bf16[1152,720]{0,1:T(8,128)(2,1)} %get-tuple-element.26) | copy-start | bytes 4976644
  466.0 11.1 %copy-start.1 = (bf16[192,720]{1,0:T(8,128)(2,1)S(1)}, bf16[192,720]{1,0:T(8,128)(2,1)}, u32[]{:S(2)}) copy-start(bf16[192,720]{1,0:T(8,128)(2,1)} %param.8) | copy-start | bytes 829444
Sparse Core Ops, SparseCore 0:
  84.4 114.7 all-gather.3
  201.0 76.5 all-gather.5
  338.8 74.3 reduce-scatter.6
